TPU v7x, 32 devices: a whole 2x2x4 slice. The times are simulated.
32 devices in a mesh: tm: 4 (over y, x), pair: 8 (over z, core).
Axes of the slice: x: 2, y: 2, z: 4, core: 2. Of those that a mesh axis runs over, the one named last changes fastest.
Arguments:
- three_center: bfloat16 [192, 64, 1024], P('pair'), may hold values from -6 to 6
- green_occ: bfloat16 [4, 64, 64, 64], P('tm'), may hold values from -0.75 to 0.75
- green_vir: bfloat16 [4, 64, 64, 64], P('tm'), may hold values from -0.75 to 0.75
- pair_list: int32 [192], P('pair'), may hold values from 0 to 63
- block_counts: int32 [8], P('pair'), may hold values from 6 to 24, as said below
- cosine_weights: float32 [4, 4], replicated, may hold values from -3 to 3
- coulomb_rows: int32 [8, 3], replicated, may hold values from 0 to 7, as said below
- coulomb_blocks: float32 [8, 3, 128, 128], replicated, may hold values from -0.3125 to 0.3125
Outputs:
- screened: float32 [4, 1024, 1024], P('tm', 'pair')
Inputs may be any that keep to these rules, and one draw needn't show every extreme that they name: `block_counts`: slots from the count on are not used; some index of pair has all 24 slots live. `coulomb_rows`: the row blocks of one column block are distinct, and the first is the column block itself.
All inputs are finite; a program needn't handle non-finite values.
Results may differ from a plain program's by a relative error of at most 0.0041.
Values sent between devices are 32-bit elements; how exact they have to be, the bound alone decides.
A program may use at most 64 MiB of HBM per device.

v0:
```python
import math
import jax
import jax.numpy as jnp
from jax import lax
from jax.sharding import PartitionSpec as P


def half_product(green_matrix, pair_list, alive_mask, three_center):
    picked = green_matrix[0][pair_list]
    product = jnp.einsum("bij,bjp->bip", picked, three_center, preferred_element_type=jnp.float32)
    product = product * alive_mask[:, None, None]
    return product.astype(jnp.bfloat16).reshape(-1, three_center.shape[2])


def local(
    three_center,
    green_occ,
    green_vir,
    pair_list,
    block_counts,
    cosine_weights,
    coulomb_rows,
    coulomb_blocks,
):
    slots = three_center.shape[0]
    pair_devices = lax.axis_size("pair")
    alive_mask = (jnp.arange(slots, dtype=jnp.int32) < block_counts[0]).astype(jnp.float32)
    left_side = half_product(green_occ, pair_list, alive_mask, three_center)
    right_side = half_product(green_vir, pair_list, alive_mask, three_center)
    normalizer = 1.0 / math.sqrt(slots * three_center.shape[1] * pair_devices)
    summed = lax.dot_general(
        left_side, right_side, (((0,), (0,)), ((), ())), preferred_element_type=jnp.float32
    )
    row_slab = lax.psum_scatter(summed * normalizer, "pair", scatter_dimension=0, tiled=True)
    transformed = jnp.einsum(
        "ft,trc->frc",
        cosine_weights,
        lax.all_to_all(row_slab[None], "tm", split_axis=2, concat_axis=0, tiled=True),
        precision=lax.Precision.HIGHEST,
    )
    spectra = lax.all_to_all(transformed, "tm", split_axis=0, concat_axis=2, tiled=True)
    rows_here = spectra.shape[1]
    column_blocks = coulomb_rows.shape[0]
    per_column = coulomb_rows.shape[1]
    block_width = coulomb_blocks.shape[2]
    blocked = spectra.reshape(rows_here, column_blocks, block_width)
    gathered = jnp.take(blocked, coulomb_rows.reshape(-1), axis=1)
    factors = coulomb_blocks.reshape(column_blocks * per_column, block_width, block_width)
    screened = jnp.einsum("mjx,jxy->mjy", gathered, factors, precision=lax.Precision.HIGHEST)
    screened = screened.reshape(rows_here, column_blocks, per_column, block_width).sum(axis=2)
    return screened.reshape(1, rows_here, column_blocks * block_width)


def solution(mesh):
    return jax.shard_map(
        local,
        mesh=mesh,
        in_specs=(
            P("pair", None, None),
            P("tm", None, None, None),
            P("tm", None, None, None),
            P("pair"),
            P("pair"),
            P(),
            P(),
            P(),
        ),
        out_specs=P("tm", "pair", None),
        check_vma=False,
    )
```

profile of v0, /device:TPU:16, one launch (start us, length us, event | category | flops | bytes accessed | tf_op | source)
XLA Modules:
  0.0 127.4 jit_solution(750855462552319083)
XLA Ops:
  6.5 0.0 copy-start
  6.5 0.0 reduce-scatter.2.cloned.1.call-start
  6.5 0.8 compare_select_fusion.1
  7.4 2.0 %gather_fusion = bf16[24,64,64]{2,1,0:T(8,128)(2,1)S(1)} fusion(bf16[64,64,64]{2,1,0:T(8,128)(2,1)} %bitcast.43, s32[1024]{0:T(1024)S(1)} %pad_clamp_fusion.1), kind=kCustom, calls=%fused_computation | custom fusion | bytes 393312 | tf_op jit(solution)/shard_map/gather | solution.py:9
  9.3 2.6 %gather_fusion.1 = bf16[24,64,64]{2,1,0:T(8,128)(2,1)} fusion(bf16[64,64,64]{2,1,0:T(8,128)(2,1)} %bitcast.44, s32[1024]{0:T(1024)S(1)} %pad_clamp_fusion.1), kind=kCustom, calls=%fused_computation.1 | custom fusion | bytes 393312 | tf_op jit(solution)/shard_map/gather | solution.py:9
  12.6 0.0 copy-done
  12.6 8.2 %bitcast_multiply_fusion = f32[1024,1024]{1,0:T(8,128)} fusion(f32[24]{0:T(128)S(1)} %compare_convert_fusion, bf16[24,64,64]{2,1,0:T(8,128)(2,1)} %gather_fusion.1, bf16[24,64,1024]{2,1,0:T(8,128)(2,1)S(1)} %copy-done, bf16[24,64,64]{2,1,0:T(8,128)(2,1)S(1)} %gather_fusion), kind=kOutput, calls=%fused_computation.5 | convolution fusion | flops 3631218688 | bytes 7733344 | tf_op jit(solution)/shard_map/dot_general | solution.py:31
  20.8 0.0 copy-start.2
  20.8 0.0 copy-start.1
  20.8 0.0 reduce-scatter.2.cloned.1.call-update
  20.9 48.7 %reduce-scatter.2.cloned.1.call-done = f32[128,1024]{1,0:T(8,128)} async-done(((f32[1024,1024]{1,0:T(8,128)}), f32[128,1024]{1,0:T(8,128)}) %reduce-scatter.2.cloned.1.call-update) | async-done | bytes 524304 | tf_op jit(solution)/shard_map/reduce_scatter | solution.py:34
  69.6 1.9 %copy.20 = f32[1,128,1024]{1,0,2:T(1,128)} copy(f32[1,128,1024]{2,1,0:T(8,128)} %bitcast.42) | data formatting | bytes 1048576 | tf_op jit(solution)/shard_map/broadcast_in_dim | solution.py:38
  71.5 4.1 %all-to-all-start = ((f32[1,128,1024]{1,0,2:T(1,128)}), f32[1,128,1024]{1,0,2:T(1,128)}, u32[]{:S(2)}, u32[]{:S(2)}) async-start(f32[1,128,1024]{1,0,2:T(1,128)} %copy.20), calls=%async_computation.1 | async-start | bytes 1048576 | tf_op jit(solution)/shard_map/all_to_all | solution.py:38
  75.6 0.0 copy-done.2
  75.6 0.1 copy.19
  75.7 0.1 reshape.61
  75.8 9.1 %all-to-all-done = f32[1,128,1024]{1,0,2:T(1,128)} async-done(((f32[1,128,1024]{1,0,2:T(1,128)}), f32[1,128,1024]{1,0,2:T(1,128)}, u32[]{:S(2)}, u32[]{:S(2)}) %all-to-all-start) | async-done | bytes 524320 | tf_op jit(solution)/shard_map/all_to_all | solution.py:38
  84.9 2.0 %copy.28 = f32[1,128,4,256]{3,2,1,0:T(4,128)} copy(f32[1,128,4,256]{1,3,2,0:T(8,128)} %bitcast.5) | data formatting | bytes 1048576 | tf_op jit(solution)/shard_map/all_to_all | solution.py:38
  87.0 0.0 copy-done.1
  87.0 2.0 %convolution_bitcast_fusion = f32[4,128,256]{2,0,1:T(4,128)S(1)} fusion(f32[1,128,4,256]{3,2,1,0:T(4,128)} %copy.28, f32[4,4]{1,0:T(4,128)S(1)} %copy-done.1), kind=kOutput, calls=%fused_computation.13 | convolution fusion | flops 6291456 | bytes 1048640 | tf_op jit(solution)/shard_map/ft,trc->frc/dot_general | solution.py:35
  89.0 0.9 copy.22
  89.9 4.1 %all-to-all-start.1 = ((f32[4,128,256]{2,1,0:T(8,128)}), f32[4,128,256]{2,1,0:T(8,128)}, u32[]{:S(2)}, u32[]{:S(2)}) async-start(f32[4,128,256]{2,1,0:T(8,128)} %copy.22), calls=%async_computation.2 | async-start | bytes 1048576 | tf_op jit(solution)/shard_map/all_to_all | solution.py:41
  94.1 0.1 reshape.59
  94.2 8.3 %all-to-all-done.1 = f32[4,128,256]{2,1,0:T(8,128)} async-done(((f32[4,128,256]{2,1,0:T(8,128)}), f32[4,128,256]{2,1,0:T(8,128)}, u32[]{:S(2)}, u32[]{:S(2)}) %all-to-all-start.1) | async-done | bytes 524320 | tf_op jit(solution)/shard_map/all_to_all | solution.py:41
  102.5 2.0 %copy.23 = f32[4,128,256]{1,2,0:T(8,128)} copy(f32[4,128,256]{2,1,0:T(8,128)} %all-to-all-done.1) | data formatting | bytes 1048576 | tf_op jit(solution)/shard_map/all_to_all | solution.py:41
  104.5 2.0 %copy.25 = f32[128,8,128]{2,0,1:T(8,128)} copy(f32[128,8,128]{0,2,1:T(8,128)} %bitcast.39) | data formatting | bytes 1048576 | tf_op jit(solution)/shard_map/reshape | solution.py:46
  106.5 2.9 %gather_fusion.2 = f32[24,128,128]{2,1,0:T(8,128)} fusion(f32[128,8,128]{2,0,1:T(8,128)} %copy.25, s32[1024]{0:T(1024)S(1)} %pad_clamp_fusion), kind=kCustom, calls=%fused_computation.2 | custom fusion | bytes 3145824 | tf_op jit(solution)/shard_map/jit(_take)/gather | solution.py:47
  109.4 4.8 %fusion.6 = f32[24,128,128]{2,1,0:T(8,128)} fusion(f32[24,128,128]{2,1,0:T(8,128)} %bitcast.41, f32[24,128,128]{2,1,0:T(8,128)} %gather_fusion.2, pred[24]{0:T(512)(128)(4,1)S(1)} %compare_and_fusion), kind=kOutput, calls=%fused_computation.10 | convolution fusion | flops 604372992 | bytes 4718616 | tf_op jit(solution)/shard_map/mjx,jxy->mjy/dot_general | solution.py:49
  114.1 2.3 %reduce_sum.9 = f32[128,8,128]{2,0,1:T(8,128)} reduce(f32[128,8,3,128]{3,0,2,1:T(8,128)} %bitcast.38, f32[]{:T(128)} %constant.22.clone.1), dimensions={2}, to_apply=%region_1.2 | reduce | flops 262144 | bytes 2097156 | tf_op jit(solution)/shard_map/reduce_sum | solution.py:50
  116.5 2.0 %copy.26 = f32[128,8,128]{0,2,1:T(8,128)} copy(f32[128,8,128]{2,0,1:T(8,128)} %reduce_sum.9) | data formatting | bytes 1048576 | tf_op jit(solution)/shard_map/reduce_sum | solution.py:50
  118.5 2.0 %copy.27 = f32[1,128,1024]{2,1,0:T(8,128)} copy(f32[1,128,1024]{1,2,0:T(8,128)} %bitcast.40) | data formatting | bytes 1048576 | tf_op jit(solution)/shard_map/reshape | solution.py:51
  (5 shorter events, 0.0 us)
Async XLA Ops:
  6.5 6.1 %copy-start = (bf16[24,64,1024]{2,1,0:T(8,128)(2,1)S(1)}, bf16[24,64,1024]{2,1,0:T(8,128)(2,1)}, u32[]{:S(2)}) copy-start(bf16[24,64,1024]{2,1,0:T(8,128)(2,1)} %param.8) | copy-start | bytes 9437188
  6.5 63.0 %reduce-scatter.2.cloned.1.call-start = ((), (), s32[]{:S(2)}) async-start(), calls=%async_computation.3 | async-start | bytes 4718592 | tf_op jit(solution)/shard_map/reduce_scatter | solution.py:34
  20.8 54.8 %copy-start.2 = (s32[8,3]{0,1:T(4,128)S(1)}, s32[8,3]{0,1:T(4,128)}, u32[]{:S(2)}) copy-start(s32[8,3]{0,1:T(4,128)} %param.14) | copy-start | bytes 292
  20.8 66.1 %copy-start.1 = (f32[4,4]{1,0:T(4,128)S(1)}, f32[4,4]{1,0:T(4,128)}, u32[]{:S(2)}) copy-start(f32[4,4]{1,0:T(4,128)} %param.13) | copy-start | bytes 196
  71.5 13.4 %all-to-all-start = ((f32[1,128,1024]{1,0,2:T(1,128)}), f32[1,128,1024]{1,0,2:T(1,128)}, u32[]{:S(2)}, u32[]{:S(2)}) async-start(f32[1,128,1024]{1,0,2:T(1,128)} %copy.20), calls=%async_computation.1 | async-start | bytes 1048576 | tf_op jit(solution)/shard_map/all_to_all | solution.py:38
  89.9 12.6 %all-to-all-start.1 = ((f32[4,128,256]{2,1,0:T(8,128)}), f32[4,128,256]{2,1,0:T(8,128)}, u32[]{:S(2)}, u32[]{:S(2)}) async-start(f32[4,128,256]{2,1,0:T(8,128)} %copy.22), calls=%async_computation.2 | async-start | bytes 1048576 | tf_op jit(solution)/shard_map/all_to_all | solution.py:41
Sparse Core Ops, SparseCore 0:
  21.0 48.5 reduce-scatter.1
where the time goes:
time: 128 us; the launch traced here: 127 us
  waiting for transfers between devices  66.1 us (52%)
  local copies, waits for them, and re-layouts  20.7 us (16%)
  matrix products  15.1 us (12%)
  between operations  14.1 us (11%)
  starting transfers between devices  8.29 us (6%)
  other arithmetic  3.18 us (2%)
    reduce_scatter x1, waiting for transfers between devices, local(): lax.psum_scatter(summed * normalizer, 'pair', scatter_dimension=0, tiled=...  48.7 us
    all_to_all x1, waiting for transfers between devices, local(): lax.all_to_all(row_slab[None], 'tm', split_axis=2, concat_axis=0, tiled=T...  9.1 us
    all_to_all x1, waiting for transfers between devices, local(): lax.all_to_all(transformed, 'tm', split_axis=0, concat_axis=2, tiled=True)  8.31 us
    dot_general x1, matrix products, local(): lax.dot_general(left_side, right_side, (((0,), (0,)), ((), ())), preferre...  8.24 us
    dot_general x1, matrix products, local(): jnp.einsum('mjx,jxy->mjy', gathered, factors, precision=lax.Precision.HIG...  4.76 us
    gather x2, local copies, waits for them, and re-layouts, half_product(): picked = green_matrix[0][pair_list]  4.56 us
    all_to_all x1, starting transfers between devices, local(): lax.all_to_all(row_slab[None], 'tm', split_axis=2, concat_axis=0, tiled=T...  4.14 us
    all_to_all x1, starting transfers between devices, local(): lax.all_to_all(transformed, 'tm', split_axis=0, concat_axis=2, tiled=True)  4.14 us
  transfers between devices with their start and end apart: 3, of which 3 were waited for; matrix products, arithmetic and copies ran while one was open for 0% of the time, Pallas kernels for 0%

commit v1 on v0

--- a/solution.py
+++ b/solution.py
@@ -3,6 +3,29 @@
 import jax.numpy as jnp
 from jax import lax
 from jax.sharding import PartitionSpec as P
+
+
+def in_blocks(shard, dim, size):
+    shape = shard.shape
+    blocks = shard.reshape(*shape[:dim], size, shape[dim] // size, *shape[dim + 1 :])
+    return jnp.moveaxis(blocks, dim, 0)
+
+
+def in_order(blocks, dim):
+    blocks = jnp.moveaxis(blocks, 0, dim)
+    lengths = blocks.shape
+    return blocks.reshape(*lengths[:dim], lengths[dim] * lengths[dim + 1], *lengths[dim + 2 :])
+
+
+def sent_to_each(x, axis, split_dim, concat_dim):
+    size, index = (lax.axis_size(axis), lax.axis_index(axis))
+    tiles = in_blocks(x, split_dim, size)
+    done = [tiles[index]]
+    for hop in range(1, size):
+        sent = tiles[(index + hop) % size]
+        done.append(lax.ppermute(sent, axis, [(i, (i + hop) % size) for i in range(size)]))
+    tiles = jnp.stack(done)[(index - jnp.arange(size)) % size]
+    return in_order(tiles, concat_dim)
 
 
 def half_product(green_matrix, pair_list, alive_mask, three_center):
@@ -38,7 +61,7 @@
         lax.all_to_all(row_slab[None], "tm", split_axis=2, concat_axis=0, tiled=True),
         precision=lax.Precision.HIGHEST,
     )
-    spectra = lax.all_to_all(transformed, "tm", split_axis=0, concat_axis=2, tiled=True)
+    spectra = sent_to_each(transformed, "tm", 0, 2)
     rows_here = spectra.shape[1]
     column_blocks = coulomb_rows.shape[0]
     per_column = coulomb_rows.shape[1]

time: 128 us -> 129 us (level)
  waiting for transfers between devices: 66.1 us -> 62.8 us
  local copies, waits for them, and re-layouts: 20.7 us -> 23.1 us
    all_to_all x1 -> x0, waiting for transfers between devices: 8.31 us -> none  [local(): lax.all_to_all(transformed, 'tm', split_axis=0, concat_axis=2, tiled=True)]
    ppermute x0 -> x3, waiting for transfers between devices: none -> 5.67 us  [sent_to_each(): lax.ppermute(sent, axis, [(i, (i + hop) % size) for i in range(size)])]
    all_to_all x1 -> x0, starting transfers between devices: 4.14 us -> none  [local(): lax.all_to_all(transformed, 'tm', split_axis=0, concat_axis=2, tiled=True)]
    ppermute x0 -> x3, starting transfers between devices: none -> 3.67 us  [sent_to_each(): lax.ppermute(sent, axis, [(i, (i + hop) % size) for i in range(size)])]
    another operation x0 -> x2, local copies, waits for them, and re-layouts: none -> 2.5 us  [the longest x1 2.04 us: local(): blocked = spectra.reshape(rows_here, column_blocks, block_width)]
    gather x0 -> x1, local copies, waits for them, and re-layouts: none -> 2.41 us  [sent_to_each(): tiles = jnp.stack(done)[(index - jnp.arange(size)) % size]]
    all_to_all x1 -> x0, local copies, waits for them, and re-layouts: 2.04 us -> none  [local(): lax.all_to_all(transformed, 'tm', split_axis=0, concat_axis=2, tiled=True)]
    transpose x0 -> x1, local copies, waits for them, and re-layouts: none -> 2.03 us  [in_order(): blocks = jnp.moveaxis(blocks, 0, dim)]
  transfers between devices with their start and end apart: 3 -> 5, of which waited for: 3 -> 4; matrix products, arithmetic and copies ran while one was open for 0% -> 0% of each run, Pallas kernels for 0% -> 0%
where the time goes in v1:
time: 129 us; the launch traced here: 127 us
  waiting for transfers between devices  62.8 us (49%)
  local copies, waits for them, and re-layouts  23.1 us (18%)
  matrix products  15.1 us (12%)
  between operations  14.3 us (11%)
  starting transfers between devices  7.81 us (6%)
  other arithmetic  4.03 us (3%)
    reduce_scatter x1, waiting for transfers between devices, local(): lax.psum_scatter(summed * normalizer, 'pair', scatter_dimension=0, tiled=...  47.8 us
    all_to_all x1, waiting for transfers between devices, local(): lax.all_to_all(row_slab[None], 'tm', split_axis=2, concat_axis=0, tiled=T...  9.27 us
    dot_general x1, matrix products, local(): lax.dot_general(left_side, right_side, (((0,), (0,)), ((), ())), preferre...  8.26 us
    ppermute x3, waiting for transfers between devices, sent_to_each(): lax.ppermute(sent, axis, [(i, (i + hop) % size) for i in range(size)])  5.67 us
    dot_general x1, matrix products, local(): jnp.einsum('mjx,jxy->mjy', gathered, factors, precision=lax.Precision.HIG...  4.77 us
    gather x2, local copies, waits for them, and re-layouts, half_product(): picked = green_matrix[0][pair_list]  4.42 us
    all_to_all x1, starting transfers between devices, local(): lax.all_to_all(row_slab[None], 'tm', split_axis=2, concat_axis=0, tiled=T...  4.14 us
    ppermute x3, starting transfers between devices, sent_to_each(): lax.ppermute(sent, axis, [(i, (i + hop) % size) for i in range(size)])  3.67 us
  transfers between devices with their start and end apart: 5, of which 4 were waited for; matrix products, arithmetic and copies ran while one was open for 0% of the time, Pallas kernels for 0%

profile of v1, /device:TPU:16, one launch (start us, length us, event | category | flops | bytes accessed | tf_op | source)
XLA Modules:
  0.0 127.1 jit_solution(13330150208264891212)
XLA Ops:
  6.5 0.0 copy-start
  6.5 0.0 reduce-scatter.2.cloned.1.call-start
  7.4 0.8 compare_select_fusion.2
  8.2 1.8 %gather_fusion.1 = bf16[24,64,64]{2,1,0:T(8,128)(2,1)S(1)} fusion(bf16[64,64,64]{2,1,0:T(8,128)(2,1)} %bitcast.61, s32[1024]{0:T(1024)S(1)} %pad_clamp_fusion.2), kind=kCustom, calls=%fused_computation.1 | custom fusion | bytes 393312 | tf_op jit(solution)/shard_map/gather | solution.py:32
  10.0 2.6 %gather_fusion = bf16[24,64,64]{2,1,0:T(8,128)(2,1)} fusion(bf16[64,64,64]{2,1,0:T(8,128)(2,1)} %bitcast.62, s32[1024]{0:T(1024)S(1)} %pad_clamp_fusion.2), kind=kCustom, calls=%fused_computation | custom fusion | bytes 393312 | tf_op jit(solution)/shard_map/gather | solution.py:32
  12.6 0.0 copy-done
  12.6 8.3 %bitcast_multiply_fusion = f32[1024,1024]{1,0:T(8,128)} fusion(f32[24]{0:T(128)S(1)} %compare_convert_fusion, bf16[24,64,64]{2,1,0:T(8,128)(2,1)S(1)} %gather_fusion.1, bf16[24,64,1024]{2,1,0:T(8,128)(2,1)S(1)} %copy-done, bf16[24,64,64]{2,1,0:T(8,128)(2,1)} %gather_fusion), kind=kOutput, calls=%fused_computation.6 | convolution fusion | flops 3631218688 | bytes 7733344 | tf_op jit(solution)/shard_map/dot_general | solution.py:54
  20.9 0.0 copy-start.2
  20.9 0.0 copy-start.1
  20.9 0.0 reduce-scatter.2.cloned.1.call-update
  20.9 0.6 copy-done.2
  21.5 0.1 copy.23
  21.6 0.1 reshape.118
  21.7 0.1 reshape.117
  21.8 47.8 %reduce-scatter.2.cloned.1.call-done = f32[128,1024]{1,0:T(8,128)} async-done(((f32[1024,1024]{1,0:T(8,128)}), f32[128,1024]{1,0:T(8,128)}) %reduce-scatter.2.cloned.1.call-update) | async-done | bytes 524304 | tf_op jit(solution)/shard_map/reduce_scatter | solution.py:57
  69.6 1.9 %copy.24 = f32[1,128,1024]{1,0,2:T(1,128)} copy(f32[1,128,1024]{2,1,0:T(8,128)} %bitcast.59) | data formatting | bytes 1048576 | tf_op jit(solution)/shard_map/broadcast_in_dim | solution.py:61
  71.5 4.1 %all-to-all-start = ((f32[1,128,1024]{1,0,2:T(1,128)}), f32[1,128,1024]{1,0,2:T(1,128)}, u32[]{:S(2)}, u32[]{:S(2)}) async-start(f32[1,128,1024]{1,0,2:T(1,128)} %copy.24), calls=%async_computation.1 | async-start | bytes 1048576 | tf_op jit(solution)/shard_map/all_to_all | solution.py:61
  75.7 9.3 %all-to-all-done = f32[1,128,1024]{1,0,2:T(1,128)} async-done(((f32[1,128,1024]{1,0,2:T(1,128)}), f32[1,128,1024]{1,0,2:T(1,128)}, u32[]{:S(2)}, u32[]{:S(2)}) %all-to-all-start) | async-done | bytes 524320 | tf_op jit(solution)/shard_map/all_to_all | solution.py:61
  85.0 2.0 %copy.31 = f32[1,128,4,256]{3,2,1,0:T(4,128)} copy(f32[1,128,4,256]{1,3,2,0:T(8,128)} %bitcast.5) | data formatting | bytes 1048576 | tf_op jit(solution)/shard_map/all_to_all | solution.py:61
  87.0 0.0 copy-done.1
  87.0 2.0 %fusion.11 = f32[128,256,4]{1,2,0:T(4,128)S(1)} fusion(f32[1,128,4,256]{3,2,1,0:T(4,128)} %copy.31, f32[4,4]{1,0:T(4,128)S(1)} %copy-done.1), kind=kOutput, calls=%fused_computation.17 | convolution fusion | flops 6291456 | bytes 1048640 | tf_op jit(solution)/shard_map/ft,trc->frc/dot_general | solution.py:58
  89.1 0.5 constant_dynamic-slice_fusion.3
  89.5 1.5 %collective-permute-start.2 = (f32[1,128,256]{2,1,0:T(8,128)S(1)}, f32[1,128,256]{2,1,0:T(8,128)S(1)}, u32[]{:S(2)}, u32[]{:S(2)}) collective-permute-start(f32[1,128,256]{2,1,0:T(8,128)S(1)} %bitcast.63), channel_id=1, source_target_pairs={{0,24},{8,0},{16,8},{24,16},{1,25},{9,1},{17,9},{25,17},{2,26},{10... | collective-permute-start | bytes 393224 | tf_op jit(solution)/shard_map/ppermute | solution.py:26
  91.0 1.5 %collective-permute-start.1 = (f32[1,128,256]{2,1,0:T(8,128)S(1)}, f32[1,128,256]{2,1,0:T(8,128)S(1)}, u32[]{:S(2)}, u32[]{:S(2)}) collective-permute-start(f32[1,128,256]{2,1,0:T(8,128)S(1)} %bitcast.64), channel_id=1, source_target_pairs={{0,16},{8,24},{16,0},{24,8},{1,17},{9,25},{17,1},{25,9},{2,18},{10... | collective-permute-start | bytes 393224 | tf_op jit(solution)/shard_map/ppermute | solution.py:26
  92.6 0.7 collective-permute-start
  93.3 2.0 %collective-permute-done.2 = f32[1,128,256]{2,1,0:T(8,128)S(1)} collective-permute-done((f32[1,128,256]{2,1,0:T(8,128)S(1)}, f32[1,128,256]{2,1,0:T(8,128)S(1)}, u32[]{:S(2)}, u32[]{:S(2)}) %collective-permute-start.2) | collective-permute-done | bytes 131104 | tf_op jit(solution)/shard_map/ppermute | solution.py:26
  95.3 3.7 %collective-permute-done.1 = f32[1,128,256]{2,1,0:T(8,128)S(1)} collective-permute-done((f32[1,128,256]{2,1,0:T(8,128)S(1)}, f32[1,128,256]{2,1,0:T(8,128)S(1)}, u32[]{:S(2)}, u32[]{:S(2)}) %collective-permute-start.1) | collective-permute-done | bytes 131104 | tf_op jit(solution)/shard_map/ppermute | solution.py:26
  98.9 0.0 collective-permute-done
  99.0 0.8 maximum_bitcast_fusion
  99.8 2.4 %gather_fusion.2 = f32[4,128,256]{2,1,0:T(8,128)} fusion(f32[4,128,256]{2,1,0:T(8,128)} %maximum_bitcast_fusion, s32[1024]{0:T(1024)S(1)} %pad_clamp_fusion.1), kind=kCustom, calls=%fused_computation.2 | custom fusion | bytes 1048592 | tf_op jit(solution)/shard_map/gather | solution.py:27
  102.2 2.0 %copy.26 = f32[1,128,4,256]{1,3,2,0:T(8,128)} copy(f32[1,128,4,256]{3,1,2,0:T(8,128)} %bitcast.55) | data formatting | bytes 1048576 | tf_op jit(solution)/shard_map/transpose | solution.py:15
  104.2 2.0 %copy.28 = f32[128,8,128]{2,0,1:T(8,128)} copy(f32[128,8,128]{0,2,1:T(8,128)} %bitcast.56) | data formatting | bytes 1048576 | tf_op jit(solution)/shard_map/reshape;reshape | solution.py:69
  106.3 2.8 %gather_fusion.3 = f32[24,128,128]{2,1,0:T(8,128)} fusion(f32[128,8,128]{2,0,1:T(8,128)} %copy.28, s32[1024]{0:T(1024)S(1)} %pad_clamp_fusion), kind=kCustom, calls=%fused_computation.3 | custom fusion | bytes 3145824 | tf_op jit(solution)/shard_map/jit(_take)/gather | solution.py:70
  109.1 4.8 %fusion.6 = f32[24,128,128]{2,1,0:T(8,128)} fusion(f32[24,128,128]{2,1,0:T(8,128)} %bitcast.58, f32[24,128,128]{2,1,0:T(8,128)} %gather_fusion.3, pred[24]{0:T(512)(128)(4,1)S(1)} %compare_and_fusion), kind=kOutput, calls=%fused_computation.11 | convolution fusion | flops 604372992 | bytes 4718616 | tf_op jit(solution)/shard_map/mjx,jxy->mjy/dot_general | solution.py:72
  113.9 2.3 %reduce_sum.9 = f32[128,8,128]{2,0,1:T(8,128)} reduce(f32[128,8,3,128]{3,0,2,1:T(8,128)} %bitcast.54, f32[]{:T(128)} %constant.63.clone.1), dimensions={2}, to_apply=%region_1.2 | reduce | flops 262144 | bytes 2097156 | tf_op jit(solution)/shard_map/reduce_sum | solution.py:73
  116.2 2.0 %copy.29 = f32[128,8,128]{0,2,1:T(8,128)} copy(f32[128,8,128]{2,0,1:T(8,128)} %reduce_sum.9) | data formatting | bytes 1048576 | tf_op jit(solution)/shard_map/reduce_sum | solution.py:73
  118.3 2.0 %copy.30 = f32[1,128,1024]{2,1,0:T(8,128)} copy(f32[1,128,1024]{1,2,0:T(8,128)} %bitcast.57) | data formatting | bytes 1048576 | tf_op jit(solution)/shard_map/reshape | solution.py:74
  (11 shorter events, 0.1 us)
Async XLA Ops:
  6.5 6.1 %copy-start = (bf16[24,64,1024]{2,1,0:T(8,128)(2,1)S(1)}, bf16[24,64,1024]{2,1,0:T(8,128)(2,1)}, u32[]{:S(2)}) copy-start(bf16[24,64,1024]{2,1,0:T(8,128)(2,1)} %param.8) | copy-start | bytes 9437188
  6.5 63.1 %reduce-scatter.2.cloned.1.call-start = ((), (), s32[]{:S(2)}) async-start(), calls=%async_computation.2 | async-start | bytes 4718592 | tf_op jit(solution)/shard_map/reduce_scatter | solution.py:57
  20.9 0.7 copy-start.2
  20.9 66.1 %copy-start.1 = (f32[4,4]{1,0:T(4,128)S(1)}, f32[4,4]{1,0:T(4,128)}, u32[]{:S(2)}) copy-start(f32[4,4]{1,0:T(4,128)} %param.13) | copy-start | bytes 196
  71.5 13.4 %all-to-all-start = ((f32[1,128,1024]{1,0,2:T(1,128)}), f32[1,128,1024]{1,0,2:T(1,128)}, u32[]{:S(2)}, u32[]{:S(2)}) async-start(f32[1,128,1024]{1,0,2:T(1,128)} %copy.24), calls=%async_computation.1 | async-start | bytes 1048576 | tf_op jit(solution)/shard_map/all_to_all | solution.py:61
  89.5 5.7 %collective-permute-start.2 = (f32[1,128,256]{2,1,0:T(8,128)S(1)}, f32[1,128,256]{2,1,0:T(8,128)S(1)}, u32[]{:S(2)}, u32[]{:S(2)}) collective-permute-start(f32[1,128,256]{2,1,0:T(8,128)S(1)} %bitcast.63), channel_id=1, source_target_pairs={{0,24},{8,0},{16,8},{24,16},{1,25},{9,1},{17,9},{25,17},{2,26},{10... | collective-permute-start | bytes 393224 | tf_op jit(solution)/shard_map/ppermute | solution.py:26
  91.0 7.9 %collective-permute-start.1 = (f32[1,128,256]{2,1,0:T(8,128)S(1)}, f32[1,128,256]{2,1,0:T(8,128)S(1)}, u32[]{:S(2)}, u32[]{:S(2)}) collective-permute-start(f32[1,128,256]{2,1,0:T(8,128)S(1)} %bitcast.64), channel_id=1, source_target_pairs={{0,16},{8,24},{16,0},{24,8},{1,17},{9,25},{17,1},{25,9},{2,18},{10... | collective-permute-start | bytes 393224 | tf_op jit(solution)/shard_map/ppermute | solution.py:26
  92.6 6.4 %collective-permute-start = (f32[1,128,256]{2,1,0:T(8,128)S(1)}, f32[1,128,256]{2,1,0:T(8,128)S(1)}, u32[]{:S(2)}, u32[]{:S(2)}) collective-permute-start(f32[1,128,256]{2,1,0:T(8,128)S(1)} %bitcast.65), channel_id=1, source_target_pairs={{0,8},{8,16},{16,24},{24,0},{1,9},{9,17},{17,25},{25,1},{2,10},{10... | collective-permute-start | bytes 393224 | tf_op jit(solution)/shard_map/ppermute | solution.py:26
Sparse Core Ops, SparseCore 0:
  21.0 48.5 reduce-scatter.1
